TPU v7x, 512 devices: a whole 4x4x16 slice. The times are simulated.
512 devices in a mesh: fsdp: 128 (over y, z_lo, x), dp: 4 (over z_hi, core).
Axes of the slice: x: 4, y: 4, z: 16 (z_hi: 2, z_lo: 8; z = z_hi * 8 + z_lo), core: 2. Of those that a mesh axis runs over, the one named last changes fastest.
Arguments:
- tokens: bfloat16 [65536, 4096], P(('fsdp', 'dp')), may hold values from -6 to 6
- norm_gain: float32 [4096], replicated, may hold values from 0.25 to 1.75
- penalty: float32 [14336], P('dp'), may hold values from 0.25 to 4
- weight_tiles: bfloat16 [4, 384, 4096], P(None, 'fsdp'), may hold values from -0.375 to 0.375
- block_rows: int32 [224, 4], replicated, may hold values from 0 to 63, as said below
- block_slot: int32 [224, 4], replicated, may hold values from 0 to 383, as said below
Outputs:
- grad_tokens: bfloat16 [65536, 4096], P(('fsdp', 'dp'))
Inputs may be any that keep to these rules, and one draw needn't show every extreme that they name: `block_rows`: each block column names 4 distinct block rows. Within each run of 56 block columns (columns q * 56 to (q + 1) * 56 - 1), a block row is named at most 4 times, and some block row exactly 4 times. `block_slot`: within each run of 56 block columns, no slot is named twice. Slot s is stored by fsdp index s // 3; in each run some fsdp index has all 3 of its slots named.
All inputs are finite; a program needn't handle non-finite values.
Results may differ from a plain program's by a relative error of at most 0.014.
Values may be sent and summed in bfloat16 or wider, within the bound.
No kernel may reach another device: no remote copies, remote signals or barrier semaphores. Data moves between devices by JAX's collectives and lax.ppermute only.
A program may use at most 128 MiB of HBM per device.

v0:
```python
import math
import jax
import jax.numpy as jnp
from jax import lax
from jax.sharding import PartitionSpec as P

BLOCK = 64


def on_device(tokens, norm_gain, penalty, weight_tiles, block_rows, block_slot):
    quarter = lax.axis_index("dp")
    model_width = tokens.shape[1]
    as_float = tokens.astype(jnp.float32)
    rms_scale = jnp.sqrt(jnp.mean(as_float * as_float, axis=1, keepdims=True) + 1e-05)
    normed = as_float / rms_scale
    scaled = (normed * norm_gain).astype(jnp.bfloat16)
    own_tiles = lax.dynamic_index_in_dim(weight_tiles, quarter, 0, keepdims=False)
    gathered = lax.all_gather(scaled, "dp", axis=0, tiled=True)
    group_rows = gathered.shape[0]
    row_blocks = model_width // BLOCK
    per_column = block_rows.shape[1]
    col_blocks = penalty.shape[0] // BLOCK
    rows_here = lax.dynamic_slice_in_dim(block_rows, quarter * col_blocks, col_blocks, 0)
    slots_here = lax.dynamic_slice_in_dim(block_slot, quarter * col_blocks, col_blocks, 0)
    entries = col_blocks * per_column
    flat_slots = slots_here.reshape(-1)
    stored = lax.all_gather(own_tiles, "fsdp", axis=0, tiled=True)
    weights_here = stored[flat_slots].reshape(entries, BLOCK, BLOCK)
    feat_blocks = gathered.T.reshape(row_blocks, BLOCK, group_rows)
    unit_scale = penalty.reshape(col_blocks, BLOCK, 1)
    col_size = math.gcd(col_blocks, 4)
    col_groups = col_blocks // col_size

    def forward_group(pieces):
        weight_group, row_group, unit_group = pieces
        selected = feat_blocks[row_group]
        preact = jnp.einsum(
            "gkio,gkin->gon", weight_group, selected, preferred_element_type=jnp.float32
        )
        gating = jax.nn.sigmoid(preact)
        grad_act = unit_group * (preact * gating)
        grad_pre = grad_act * (gating * (1.0 + preact * (1.0 - gating)))
        return grad_pre.astype(jnp.bfloat16)

    grad_pre = lax.map(
        forward_group,
        (
            weights_here.reshape(col_groups, col_size, per_column, BLOCK, BLOCK),
            rows_here.reshape(col_groups, col_size, per_column),
            unit_scale.reshape(col_groups, col_size, BLOCK, 1),
        ),
    )
    grad_pre = grad_pre.reshape(col_blocks, BLOCK, group_rows)
    row_cap = -(-entries // row_blocks)
    flat_rows = rows_here.reshape(-1)
    row_hits = (flat_rows[:, None] == jnp.arange(row_blocks, dtype=jnp.int32)[None, :]).astype(
        jnp.int32
    )
    hits_before = jnp.cumsum(row_hits, axis=0) - row_hits
    row_rank = jnp.sum(hits_before * row_hits, axis=1)
    slot_table = jnp.full((row_blocks * row_cap,), entries, jnp.int32)
    slot_table = slot_table.at[flat_rows * row_cap + row_rank].set(
        jnp.arange(entries, dtype=jnp.int32)
    )
    padded_tiles = jnp.concatenate([weights_here, jnp.zeros((1, BLOCK, BLOCK), jnp.bfloat16)], 0)
    back_tiles = padded_tiles[slot_table].reshape(row_blocks, row_cap, BLOCK, BLOCK)
    back_columns = jnp.where(slot_table < entries, slot_table // per_column, 0).reshape(
        row_blocks, row_cap
    )
    row_size = math.gcd(row_blocks, 4)
    row_groups = row_blocks // row_size
    grad_part = grad_pre

    def one_group(pieces):
        tile_group, column_group = pieces
        selected = grad_part[column_group]
        return jnp.einsum(
            "gqio,gqon->ngi", tile_group, selected, preferred_element_type=jnp.float32
        )

    grouped = lax.map(
        one_group,
        (
            back_tiles.reshape(row_groups, row_size, row_cap, BLOCK, BLOCK),
            back_columns.reshape(row_groups, row_size, row_cap),
        ),
    )
    summed = lax.psum_scatter(
        grouped.transpose(1, 0, 2, 3).reshape(group_rows, model_width).astype(jnp.bfloat16),
        "dp",
        scatter_dimension=0,
        tiled=True,
    ).astype(jnp.float32)
    grad_norm = summed * norm_gain
    mixing = jnp.mean(grad_norm * normed, axis=1, keepdims=True)
    return ((grad_norm - normed * mixing) / rms_scale).astype(jnp.bfloat16)


def solution(mesh):
    placed = (P(("fsdp", "dp"), None), P(), P("dp"), P(None, "fsdp", None), P(), P())
    return jax.shard_map(
        on_device, mesh=mesh, in_specs=placed, out_specs=P(("fsdp", "dp"), None), check_vma=False
    )
```

profile of v0, /device:TPU:1, one launch (start us, length us, event | category | flops | bytes accessed | tf_op | source)
XLA Modules:
  0.0 1400.3 jit_solution(17715397416254381017)
XLA Ops:
  16.2 877.6 %all-gather.6.cloned.1.call-done = bf16[1,384,4096]{2,0,1:T(2,128)(2,1)} async-done(((bf16[1,3,4096]{2,0,1:T(2,128)(2,1)}), bf16[1,384,4096]{2,0,1:T(2,128)(2,1)}) %all-gather.6.cloned.1.call-update) | async-done | bytes 3145744 | tf_op jit(solution)/shard_map/all_gather | solution.py:27
  893.8 6.3 copy.69
  900.2 2.9 gather_fusion.2
  903.1 4.1 copy.55
  907.2 4.9 reshape_reshape.14
  912.1 5.6 copy.56
  917.8 4.9 concatenate.3
  922.6 5.1 gather_fusion.3
  927.7 174.2 %all-gather.4.cloned.1.call-done = bf16[512,4096]{0,1:T(8,128)(2,1)} async-done(((bf16[128,4096]{0,1:T(8,128)(2,1)}), bf16[512,4096]{0,1:T(8,128)(2,1)}) %all-gather.4.cloned.1.call-update) | async-done | bytes 4194320 | tf_op jit(solution)/shard_map/all_gather | solution.py:18
  1101.9 70.7 %while.20 = (s32[]{:T(128)}, bf16[14,4,64,512]{3,2,1,0:T(8,128)(2,1)}, f32[14,4,64,1]{2,1,3,0:T(4,128)S(1)}, bf16[14,4,4,64,64]{4,3,2,1,0:T(8,128)(2,1)}, s32[14...) while((s32[]{:T(128)}, bf16[14,4,64,512]{3,2,1,0:T(8,128)(2,1)}, ...), condition=%wide.region_6.7_spmd, body=%wide.region_5.6_spmd.sunk | while | flops 68551728 | bytes 3678677 | solution.py:45
  1102.0 2.8 gather_fusion
  1107.1 2.8 gather_fusion
  1112.2 2.8 gather_fusion
  1117.2 2.8 gather_fusion
  1122.3 2.8 gather_fusion
  1127.3 2.8 gather_fusion
  1132.3 2.8 gather_fusion
  1137.4 2.8 gather_fusion
  1142.4 2.8 gather_fusion
  1147.5 2.8 gather_fusion
  1152.5 2.8 gather_fusion
  1157.5 2.8 gather_fusion
  1162.6 2.8 gather_fusion
  1167.7 2.8 gather_fusion
  1172.6 76.2 %while.21 = (s32[]{:T(128)}, bf16[16,512,4,64]{1,3,2,0:T(8,128)(2,1)}, s32[16,4,4]{2,1,0:T(4,128)S(1)}, bf16[56,64,512]{2,1,0:T(8,128)(2,1)}, bf16[16,4,4,64,64]{4,3,2,1,0:T(8,128)(2,1)}, /*index=5*/s32[]{:T(128)}) while((s32[]{:T(128)}, bf16[16,512,4,64]{1,3,2,0:T(8,128)(2,1)}, s32[16,4,4]{2,1,0:T(4,128)S(1)}, ...), condition=%wide.region_8.9_spmd, body=%wide.region_7.8_spmd.sunk | while | flops 67109936 | bytes 3937737 | solution.py:81
  1172.7 2.7 gather_fusion.1
  1177.5 2.7 gather_fusion.1
  1182.2 2.7 gather_fusion.1
  1187.0 2.7 gather_fusion.1
  1191.8 2.7 gather_fusion.1
  1248.8 6.4 copy.60
  1255.3 134.1 %reduce-scatter.4.cloned.1.call-done = bf16[128,4096]{1,0:T(8,128)(2,1)} async-done(((bf16[512,4096]{1,0:T(8,128)(2,1)}), bf16[128,4096]{1,0:T(8,128)(2,1)}) %reduce-scatter.4.cloned.1.call-update) | async-done | bytes 1048592
  (203 shorter events, 107.9 us)
Async XLA Ops:
  6.5 0.9 copy-start
  6.5 6.1 copy-start.6
  6.5 7.5 copy-start.7
  6.5 7.8 copy-start.5
  6.5 887.3 %all-gather.6.cloned.1.call-start = ((), (), s32[]{:S(2)}) async-start(), calls=%async_computation.2 | async-start | bytes 6340608 | tf_op jit(solution)/shard_map/all_gather | solution.py:27
  8.1 1093.8 %all-gather.4.cloned.1.call-start = ((), (), s32[]{:S(2)}) async-start(), calls=%async_computation.1 | async-start | bytes 5242880 | tf_op jit(solution)/shard_map/all_gather | solution.py:18
  9.8 6.4 copy-start.1
  12.6 1376.8 %reduce-scatter.4.cloned.1.call-start = ((), (), s32[]{:S(2)}) async-start(), calls=%async_computation.3 | async-start | bytes 5242880
  903.1 4.1 copy-start.3
  1255.2 135.8 %copy-start.2 = (bf16[128,4096]{0,1:T(8,128)(2,1)S(1)}, bf16[128,4096]{0,1:T(8,128)(2,1)}, u32[]{:S(2)}) copy-start(bf16[128,4096]{0,1:T(8,128)(2,1)} %copy-done.1) | copy-start | bytes 3145732
  1255.2 135.8 %copy-start.4 = (f32[4096]{0:T(1024)S(1)}, f32[4096]{0:T(1024)}, u32[]{:S(2)}) copy-start(f32[4096]{0:T(1024)} %param.11) | copy-start | bytes 49156
Sparse Core Ops, SparseCore 0:
  9.4 884.3 all-gather.5
  895.9 205.9 all-gather.3
  1255.4 133.9 reduce-scatter.3
where the time goes:
time: 1400 us
  waiting for transfers between devices  1190 us (85%)
  local copies, waits for them, and re-layouts  133 us (10%)
  matrix products  61.8 us (4%)
    all_gather x1, waiting for transfers between devices, on_device(): stored = lax.all_gather(own_tiles, 'fsdp', axis=0, tiled=True)  878 us
    all_gather x1, waiting for transfers between devices, on_device(): gathered = lax.all_gather(scaled, 'dp', axis=0, tiled=True)  174 us
    unnamed x4, waiting for transfers between devices  134 us
    gather x16, local copies, waits for them, and re-layouts, one_group(): selected = grad_part[column_group]  42.4 us
    gather x14, local copies, waits for them, and re-layouts, forward_group(): selected = feat_blocks[row_group]  39.2 us
    dot_general x16, matrix products, one_group(): jnp.einsum('gqio,gqon->ngi', tile_group, selected, preferred_element_type...  32.1 us
    dot_general x14, matrix products, forward_group(): jnp.einsum('gkio,gkin->gon', weight_group, selected, preferred_element_ty...  29.7 us
  transfers between devices with their start and end apart: 3, of which 3 were waited for; matrix products, arithmetic and copies ran while one was open for 3% of the time, Pallas kernels for 0%

commit v1 on v0

--- a/solution.py
+++ b/solution.py
@@ -24,7 +24,9 @@
     slots_here = lax.dynamic_slice_in_dim(block_slot, quarter * col_blocks, col_blocks, 0)
     entries = col_blocks * per_column
     flat_slots = slots_here.reshape(-1)
-    stored = lax.all_gather(own_tiles, "fsdp", axis=0, tiled=True)
+    stored = jnp.concatenate(
+        lax.all_to_all(jnp.stack([own_tiles] * lax.axis_size("fsdp")), "fsdp", 0, 0), axis=0
+    )
     weights_here = stored[flat_slots].reshape(entries, BLOCK, BLOCK)
     feat_blocks = gathered.T.reshape(row_blocks, BLOCK, group_rows)
     unit_scale = penalty.reshape(col_blocks, BLOCK, 1)

time: 1400 us -> 648 us (0.46)
  waiting for transfers between devices: 1190 us -> 408 us
  starting transfers between devices: 0.12 us -> 21.1 us
    all_gather x1 -> x0, waiting for transfers between devices: 878 us -> none  [on_device(): stored = lax.all_gather(own_tiles, 'fsdp', axis=0, tiled=True)]
    all_to_all x0 -> x1, waiting for transfers between devices: none -> 267 us  [on_device(): lax.all_to_all(jnp.stack([own_tiles] * lax.axis_size('fsdp')), 'fsdp', 0, 0)]
    all_gather x1, waiting for transfers between devices: 174 us -> 0.01 us  [on_device(): gathered = lax.all_gather(scaled, 'dp', axis=0, tiled=True)]
    all_to_all x0 -> x1, starting transfers between devices: none -> 21.1 us  [on_device(): lax.all_to_all(jnp.stack([own_tiles] * lax.axis_size('fsdp')), 'fsdp', 0, 0)]
    unnamed x4 -> x3, waiting for transfers between devices: 134 us -> 141 us
  transfers between devices with their start and end apart: 3 -> 3, of which waited for: 3 -> 2; matrix products, arithmetic and copies ran while one was open for 3% -> 5% of each run, Pallas kernels for 0% -> 0%
where the time goes in v1:
time: 648 us; the launch traced here: 645 us
  waiting for transfers between devices  408 us (63%)
  local copies, waits for them, and re-layouts  136 us (21%)
  matrix products  61.8 us (10%)
  starting transfers between devices  21.1 us (3%)
  between operations  13.7 us (2%)
    all_to_all x1, waiting for transfers between devices, on_device(): lax.all_to_all(jnp.stack([own_tiles] * lax.axis_size('fsdp')), 'fsdp', 0, 0)  267 us
    unnamed x3, waiting for transfers between devices  141 us
    gather x16, local copies, waits for them, and re-layouts, one_group(): selected = grad_part[column_group]  42.4 us
    gather x14, local copies, waits for them, and re-layouts, forward_group(): selected = feat_blocks[row_group]  39.2 us
    dot_general x16, matrix products, one_group(): jnp.einsum('gqio,gqon->ngi', tile_group, selected, preferred_element_type...  32.1 us
    dot_general x14, matrix products, forward_group(): jnp.einsum('gkio,gkin->gon', weight_group, selected, preferred_element_ty...  29.7 us
    all_to_all x1, starting transfers between devices, on_device(): lax.all_to_all(jnp.stack([own_tiles] * lax.axis_size('fsdp')), 'fsdp', 0, 0)  21.1 us
  transfers between devices with their start and end apart: 3, of which 2 were waited for; matrix products, arithmetic and copies ran while one was open for 5% of the time, Pallas kernels for 0%

profile of v1, /device:TPU:1, one launch (start us, length us, event | category | flops | bytes accessed | tf_op | source)
XLA Modules:
  0.0 645.5 jit_solution(2716023402803928321)
XLA Ops:
  7.5 4.0 stack.2
  11.6 21.1 %all-to-all-start = ((bf16[128,3,4096]{2,1,0:T(4,128)(2,1)}), bf16[128,3,4096]{2,1,0:T(4,128)(2,1)}, u32[]{:S(2)}, u32[]{:S(2)}) async-start(bf16[128,3,4096]{2,1,0:T(4,128)(2,1)} %stack.2), calls=%async_computation | async-start | bytes 8388608 | tf_op jit(solution)/shard_map/all_to_all | solution.py:28
  39.1 267.2 %all-to-all-done = bf16[128,3,4096]{2,1,0:T(4,128)(2,1)} async-done(((bf16[128,3,4096]{2,1,0:T(4,128)(2,1)}), bf16[128,3,4096]{2,1,0:T(4,128)(2,1)}, u32[]{:S(2)}, u32[]{:S(2)}) %all-to-all-start) | async-done | bytes 3145760 | tf_op jit(solution)/shard_map/all_to_all | solution.py:28
  306.4 6.0 reshape.162
  312.3 2.9 gather_fusion.2
  315.3 4.1 copy.41
  319.4 4.9 reshape_reshape.14
  324.3 5.6 copy.42
  329.9 70.7 %while.20 = (s32[]{:T(128)}, bf16[14,4,64,512]{3,2,1,0:T(8,128)(2,1)}, f32[14,4,64,1]{2,1,3,0:T(4,128)S(1)}, bf16[14,4,4,64,64]{4,3,2,1,0:T(8,128)(2,1)}, s32[14...) while((s32[]{:T(128)}, bf16[14,4,64,512]{3,2,1,0:T(8,128)(2,1)}, ...), condition=%wide.region_6.7_spmd, body=%wide.region_5.6_spmd.sunk | while | flops 68551728 | bytes 3678677 | solution.py:47
  330.0 2.8 gather_fusion
  335.1 2.8 gather_fusion
  340.1 2.8 gather_fusion
  345.2 2.8 gather_fusion
  350.2 2.8 gather_fusion
  355.3 2.8 gather_fusion
  360.3 2.8 gather_fusion
  365.4 2.8 gather_fusion
  370.4 2.8 gather_fusion
  375.5 2.8 gather_fusion
  380.5 2.8 gather_fusion
  385.5 2.8 gather_fusion
  390.6 2.8 gather_fusion
  395.7 2.8 gather_fusion
  400.6 4.9 concatenate.3
  405.5 5.1 gather_fusion.3
  410.6 76.2 %while.21 = (s32[]{:T(128)}, bf16[16,512,4,64]{1,3,2,0:T(8,128)(2,1)}, s32[16,4,4]{2,1,0:T(4,128)S(1)}, bf16[56,64,512]{2,1,0:T(8,128)(2,1)}, bf16[16,4,4,64,64]{4,3,2,1,0:T(8,128)(2,1)}, /*index=5*/s32[]{:T(128)}) while((s32[]{:T(128)}, bf16[16,512,4,64]{1,3,2,0:T(8,128)(2,1)}, s32[16,4,4]{2,1,0:T(4,128)S(1)}, ...), condition=%wide.region_8.9_spmd, body=%wide.region_7.8_spmd.sunk | while | flops 67109936 | bytes 3937737 | solution.py:83
  410.7 2.7 gather_fusion.1
  415.5 2.7 gather_fusion.1
  420.2 2.7 gather_fusion.1
  425.0 2.7 gather_fusion.1
  486.8 6.5 %copy.46 = bf16[512,4096]{1,0:T(8,128)(2,1)} copy(bf16[512,4096]{0,1:T(8,128)(2,1)} %bitcast.102) | data formatting | bytes 8388608
  493.3 140.9 %reduce-scatter.4.cloned.1.call-done = bf16[128,4096]{1,0:T(8,128)(2,1)} async-done(((bf16[512,4096]{1,0:T(8,128)(2,1)}), bf16[128,4096]{1,0:T(8,128)(2,1)}) %reduce-scatter.4.cloned.1.call-update) | async-done | bytes 1048592
  (206 shorter events, 108.4 us)
Async XLA Ops:
  6.5 0.9 copy-start
  11.6 21.1 %copy-start.4 = (bf16[128,4096]{1,0:T(8,128)(2,1)S(1)}, bf16[128,4096]{1,0:T(8,128)(2,1)}, u32[]{:S(2)}) copy-start(bf16[128,4096]{1,0:T(8,128)(2,1)} %param.10) | copy-start | bytes 3145732
  11.6 22.4 %copy-start.5 = (f32[4096]{0:T(1024)S(1)}, f32[4096]{0:T(1024)}, u32[]{:S(2)}) copy-start(f32[4096]{0:T(1024)} %param.11) | copy-start | bytes 49156
  11.6 294.8 %all-to-all-start = ((bf16[128,3,4096]{2,1,0:T(4,128)(2,1)}), bf16[128,3,4096]{2,1,0:T(4,128)(2,1)}, u32[]{:S(2)}, u32[]{:S(2)}) async-start(bf16[128,3,4096]{2,1,0:T(4,128)(2,1)} %stack.2), calls=%async_computation | async-start | bytes 8388608 | tf_op jit(solution)/shard_map/all_to_all | solution.py:28
  32.6 2.9 copy-start.7
  32.7 4.3 copy-start.8
  32.7 4.6 copy-start.6
  32.7 297.2 %all-gather.2.cloned.1.call-start = ((), (), s32[]{:S(2)}) async-start(), calls=%async_computation.2 | async-start | bytes 5242880 | tf_op jit(solution)/shard_map/all_gather | solution.py:18
  33.4 5.7 copy-start.1
  35.5 598.7 %reduce-scatter.4.cloned.1.call-start = ((), (), s32[]{:S(2)}) async-start(), calls=%async_computation.3 | async-start | bytes 5242880
  315.3 4.1 copy-start.3
  493.3 142.6 %copy-start.2 = (bf16[128,4096]{0,1:T(8,128)(2,1)S(1)}, bf16[128,4096]{0,1:T(8,128)(2,1)}, u32[]{:S(2)}) copy-start(bf16[128,4096]{0,1:T(8,128)(2,1)} %copy-done.1) | copy-start | bytes 3145732
Sparse Core Ops, SparseCore 0:
  35.6 108.6 all-gather.1
  493.5 140.7 reduce-scatter.3
